TPU v7x, 256 devices: a whole 4x4x8 slice. The times are simulated.
256 devices in a mesh: expert: 64 (over z, y, core), replica: 4 (over x).
Axes of the slice: x: 4, y: 4, z: 8, core: 2. Of those that a mesh axis runs over, the one named last changes fastest.
Arguments:
- hidden_first: bfloat16 [2048, 4096], P(('expert', 'replica')), may hold values from -40 to 40
- hidden_second: bfloat16 [2048, 4096], P(('expert', 'replica')), may hold values from -40 to 40
- routes_first: int32 [2048, 8], P(('expert', 'replica')), may hold values from 0 to 63, all different within a row; in each aligned block of 8 rows (0 to 7, 8 to 15, ...) at most 2 rows name the same one
- routes_second: int32 [2048, 8], P(('expert', 'replica')), may hold values from 0 to 63, all different within a row; in each aligned block of 8 rows (0 to 7, 8 to 15, ...) at most 2 rows name the same one
- mixing_first: float32 [2048, 8], P(('expert', 'replica')), may hold values from 0.05 to 0.5
- mixing_second: float32 [2048, 8], P(('expert', 'replica')), may hold values from 0.05 to 0.5
- norm_gain: float32 [4096], replicated, may hold values from 0.1 to 1.9
- expert_owner: int32 [64], replicated, may hold values from 0 to 63, each once
- swap_flags: int32 [64], replicated, may hold values from 0 to 1, as said below
- gate_up_values: bfloat16 [64, 2, 4096, 1024], P('expert', None, None, 'replica'), may hold values from -0.09375 to 0.09375
- gate_up_scales: bfloat16 [64, 2, 32, 8], P('expert', None, None, 'replica'), may hold values from 0.5 to 2
- down_values: bfloat16 [64, 1024, 4096], P('expert', 'replica'), may hold values from -0.1875 to 0.1875
- down_scales: bfloat16 [64, 8, 32], P('expert', 'replica'), may hold values from 0.5 to 2
Outputs:
- output_first: bfloat16 [2048, 4096], P(('expert', 'replica'))
- output_second: bfloat16 [2048, 4096], P(('expert', 'replica'))
- gate_up_moved: bfloat16 [64, 2, 4096, 1024], P('expert', None, None, 'replica')
- gate_up_scales_moved: bfloat16 [64, 2, 32, 8], P('expert', None, None, 'replica')
- down_moved: bfloat16 [64, 1024, 4096], P('expert', 'replica')
- down_scales_moved: bfloat16 [64, 8, 32], P('expert', 'replica')
Inputs may be any that keep to these rules, and one draw needn't show every extreme that they name: swap_flags[d] equals swap_flags[(d + 32) mod 64].
All inputs are finite; a program needn't handle non-finite values.
Results may differ from a plain program's by a relative error of at most 0.012.
Values may be sent and summed in bfloat16 or wider, within the bound.
No kernel may reach another device: no remote copies, remote signals or barrier semaphores. Data moves between devices by JAX's collectives and lax.ppermute only.
A program may use at most 128 MiB of HBM per device.

v0:
```python
import jax
import jax.numpy as jnp
from jax import lax
from jax.sharding import PartitionSpec as P


def partner(block, axis, bit):
    count = lax.axis_size(axis)
    route = []
    for low in range(count):
        high = low | 1 << bit
        if high != low and high < count:
            route += [(low, high), (high, low)]
    return lax.ppermute(block, axis, route)


def dequantize(values, scales):
    height, breadth = (values.shape[-2], values.shape[-1])
    block_rows, block_cols = (scales.shape[-2], scales.shape[-1])
    leading = values.shape[:-2]
    blocked = values.astype(jnp.float32).reshape(
        leading + (block_rows, height // block_rows, block_cols, breadth // block_cols)
    )
    scaled = blocked * scales.astype(jnp.float32)[..., :, None, :, None]
    return scaled.reshape(values.shape).astype(jnp.bfloat16)


def rms_normed(hidden, norm_gain):
    widened = hidden.astype(jnp.float32)
    inverse_rms = lax.rsqrt(jnp.mean(widened * widened, axis=-1, keepdims=True) + 1e-06)
    return (widened * inverse_rms * norm_gain).astype(jnp.bfloat16)


def rounded(partial_sum):
    return lax.optimization_barrier(partial_sum.astype(jnp.bfloat16)).astype(jnp.float32)


def expert_partial(token_rows, weights):
    gate_up, down_proj = weights
    gate_act = jnp.dot(token_rows, gate_up[0], preferred_element_type=jnp.float32)
    up_act = jnp.dot(token_rows, gate_up[1], preferred_element_type=jnp.float32)
    inner_act = (jax.nn.silu(gate_act) * up_act).astype(jnp.bfloat16)
    return rounded(jnp.dot(inner_act, down_proj, preferred_element_type=jnp.float32))


def pick_slots(routes, owner_slots, experts, capacity):
    tokens_here, top_count = routes.shape
    expert_ids = jnp.arange(owner_slots.shape[0], dtype=jnp.int32)
    target = jnp.sum(jnp.where(routes[:, :, None] == expert_ids, owner_slots, 0), axis=-1).reshape(
        -1
    )
    device_ids = jnp.arange(experts, dtype=jnp.int32)
    target_hot = (target[:, None] == device_ids).astype(jnp.int32)
    earlier = jnp.cumsum(target_hot, axis=0) - target_hot
    rank_in = jnp.sum(earlier * target_hot, axis=1)
    slot_ids = target * capacity + rank_in
    columns = jnp.arange(experts * capacity, dtype=jnp.int32)
    return (
        (slot_ids[:, None] == columns)
        .astype(jnp.float32)
        .reshape(tokens_here, top_count, experts * capacity)
    )


def finish(partial_terms):
    summed = lax.psum_scatter(
        partial_terms.astype(jnp.bfloat16), "replica", scatter_dimension=0, tiled=True
    )
    return lax.all_to_all(summed, "expert", split_axis=1, concat_axis=1, tiled=True)


def decode_step(hidden, routes, mixing, norm_gain, owner_slots, weights):
    experts = lax.axis_size("expert")
    copies = lax.axis_size("replica")
    tokens_here, top_count = routes.shape
    features = hidden.shape[1]
    capacity = min(tokens_here, max(2, 2 * tokens_here * top_count // experts))
    normed = rms_normed(hidden, norm_gain)
    own_picks = pick_slots(routes, owner_slots, experts, capacity)
    pooled, pooled_routes = (
        lax.all_gather(normed, "replica", axis=0, tiled=True),
        lax.all_gather(routes, "replica", axis=0, tiled=True),
    )
    grouped = pooled_routes.reshape(copies, tokens_here, top_count)
    pick_table = jax.vmap(
        lambda route_group: pick_slots(route_group, owner_slots, experts, capacity)
    )(grouped)
    placing = jnp.sum(pick_table, axis=2).astype(jnp.bfloat16)
    outgoing = jnp.einsum(
        "rts,rtd->rsd",
        placing,
        pooled.reshape(copies, tokens_here, features),
        preferred_element_type=jnp.float32,
    )
    outgoing = outgoing.astype(jnp.bfloat16).reshape(copies, experts, capacity, features)
    arrived = lax.all_to_all(outgoing, "expert", split_axis=1, concat_axis=1, tiled=True)
    slot_count = arrived.shape[2]
    flat_rows = arrived.reshape(-1, features)
    partial_terms = expert_partial(flat_rows, weights).reshape(
        copies, experts, slot_count, features
    )
    returned = finish(partial_terms)
    mixing_matrix = jnp.einsum("tks,tk->ts", own_picks, mixing, precision=lax.Precision.HIGHEST)
    merged = jnp.dot(
        mixing_matrix,
        returned.reshape(experts * capacity, features).astype(jnp.float32),
        precision=lax.Precision.HIGHEST,
    )
    return merged.astype(jnp.bfloat16)


def body(
    hidden_first,
    hidden_second,
    routes_first,
    routes_second,
    mixing_first,
    mixing_second,
    norm_gain,
    expert_owner,
    swap_flags,
    gate_up_values,
    gate_up_scales,
    down_values,
    down_scales,
):
    experts = lax.axis_size("expert")
    halfway = experts // 2
    my_slot = lax.axis_index("expert")
    current = (gate_up_values, gate_up_scales, down_values, down_scales)
    incoming = partner(
        (gate_up_values, gate_up_scales, down_values, down_scales),
        "expert",
        experts.bit_length() - 2,
    )
    slot_ids = jnp.arange(experts, dtype=jnp.int32)
    flagged = jnp.sum(jnp.where(slot_ids == my_slot, swap_flags, 0)) == 1
    moved_arrays = tuple(
        (
            jnp.where(flagged, fresh_piece, stale_piece)
            for fresh_piece, stale_piece in zip(incoming, current)
        )
    )
    weights_before = (
        dequantize(gate_up_values[0], gate_up_scales[0]),
        dequantize(down_values[0], down_scales[0]),
    )
    output_first = decode_step(
        hidden_first, routes_first, mixing_first, norm_gain, expert_owner, weights_before
    )
    owner_flags = jnp.sum(jnp.where(expert_owner[:, None] == slot_ids, swap_flags, 0), axis=1)
    owner_after = jnp.where(owner_flags == 1, (expert_owner + halfway) % experts, expert_owner)
    weights_after = (
        dequantize(moved_arrays[0][0], moved_arrays[1][0]),
        dequantize(moved_arrays[2][0], moved_arrays[3][0]),
    )
    output_second = decode_step(
        hidden_second, routes_second, mixing_second, norm_gain, owner_after, weights_after
    )
    return (
        output_first,
        output_second,
        moved_arrays[0],
        moved_arrays[1],
        moved_arrays[2],
        moved_arrays[3],
    )


def solution(mesh):
    return jax.shard_map(
        body,
        mesh=mesh,
        in_specs=(
            P(("expert", "replica"), None),
            P(("expert", "replica"), None),
            P(("expert", "replica"), None),
            P(("expert", "replica"), None),
            P(("expert", "replica"), None),
            P(("expert", "replica"), None),
            P(),
            P(),
            P(),
            P("expert", None, None, "replica"),
            P("expert", None, None, "replica"),
            P("expert", "replica", None),
            P("expert", "replica", None),
        ),
        out_specs=(
            P(("expert", "replica"), None),
            P(("expert", "replica"), None),
            P("expert", None, None, "replica"),
            P("expert", None, None, "replica"),
            P("expert", "replica", None),
            P("expert", "replica", None),
        ),
        check_vma=False,
    )
```

profile of v0, /device:TPU:1, one launch (start us, length us, event | category | flops | bytes accessed | tf_op | source)
XLA Modules:
  0.0 738.2 jit_solution(4624766096503249148)
XLA Ops:
  8.7 10.4 %all_gather.14 = s32[32,8]{1,0:T(8,128)S(1)} all-gather(s32[8,8]{1,0:T(8,128)} %param.16), channel_id=1, replica_groups=mesh['expert'=64,'replica'=4] {'replica'}, dimensions={0}, use_global_device_ids=true | all-gather | bytes 1280 | tf_op jit(solution)/shard_map/all_gather | solution.py:82
  20.6 1.0 fusion.23
  21.6 1.0 fusion.26
  22.6 1.0 fusion.28
  23.6 9.4 %all_gather.15 = bf16[32,4096]{1,0:T(8,128)(2,1)S(1)} all-gather(bf16[8,4096]{1,0:T(8,128)(2,1)S(1)} %get-tuple-element.13), channel_id=1, replica_groups=mesh['expert'=64,'replica'=4] {'replica'}, dimensions={0}, use_global_device_ids=true | all-gather | bytes 327680 | tf_op jit(solution)/shard_map/all_gather | solution.py:81
  33.0 3.3 convolution_convert_fusion.1
  36.3 7.6 %reshape.189 = bf16[4,64,2,4096]{3,2,1,0:T(2,128)(2,1)} reshape(bf16[4,128,4096]{2,1,0:T(8,128)(2,1)} %convolution_convert_fusion.1) | data formatting | bytes 8388608 | tf_op jit(solution)/shard_map/reshape | solution.py:95
  43.9 10.2 %copy.44 = bf16[4,64,2,4096]{3,2,0,1:T(2,128)(2,1)} copy(bf16[4,64,2,4096]{3,2,1,0:T(2,128)(2,1)} %reshape.189) | data formatting | bytes 8388608 | tf_op jit(solution)/shard_map/reshape | solution.py:95
  54.1 18.4 %all-to-all-start.2 = ((bf16[4,64,2,4096]{3,2,0,1:T(2,128)(2,1)}), bf16[4,64,2,4096]{3,2,0,1:T(2,128)(2,1)}, u32[]{:S(2)}, u32[]{:S(2)}) async-start(bf16[4,64,2,4096]{3,2,0,1:T(2,128)(2,1)} %copy.44), calls=%async_computation.3 | async-start | bytes 8388608 | tf_op jit(solution)/shard_map/all_to_all | solution.py:96
  72.6 5.5 collective-permute-start
  78.2 5.3 collective-permute-start.1
  83.5 10.1 %all_gather.12 = s32[32,8]{1,0:T(8,128)S(1)} all-gather(s32[8,8]{1,0:T(8,128)S(1)} %copy-done.4), channel_id=1, replica_groups=mesh['expert'=64,'replica'=4] {'replica'}, dimensions={0}, use_global_device_ids=true | all-gather | bytes 1280 | tf_op jit(solution)/shard_map/all_gather | solution.py:82
  94.9 10.6 %all_gather.13 = bf16[32,4096]{1,0:T(8,128)(2,1)S(1)} all-gather(bf16[8,4096]{1,0:T(8,128)(2,1)S(1)} %get-tuple-element.14), channel_id=1, replica_groups=mesh['expert'=64,'replica'=4] {'replica'}, dimensions={0}, use_global_device_ids=true | all-gather | bytes 327680 | tf_op jit(solution)/shard_map/all_gather | solution.py:81
  105.6 3.3 convolution_convert_fusion.3
  108.9 7.8 %reshape.185 = bf16[4,64,2,4096]{3,2,1,0:T(2,128)(2,1)} reshape(bf16[4,128,4096]{2,1,0:T(8,128)(2,1)} %convolution_convert_fusion.3) | data formatting | bytes 8388608 | tf_op jit(solution)/shard_map/reshape | solution.py:95
  116.8 10.2 %copy.39 = bf16[4,64,2,4096]{3,2,0,1:T(2,128)(2,1)} copy(bf16[4,64,2,4096]{3,2,1,0:T(2,128)(2,1)} %reshape.185) | data formatting | bytes 8388608 | tf_op jit(solution)/shard_map/reshape | solution.py:95
  128.2 243.6 %collective-permute-done.3 = bf16[1,2,32]{2,1,0:T(2,128)(2,1)S(1)} collective-permute-done((bf16[1,2,32]{2,1,0:T(2,128)(2,1)S(1)}, bf16[1,2,32]{2,1,0:T(2,128)(2,1)S(1)}, u32[]{:S(2)}, u32[]{:S(2)}) %collective-permute-start.3) | collective-permute-done | bytes 160 | tf_op jit(solution)/shard_map/ppermute | solution.py:14
  373.0 5.4 mul.142
  378.5 11.5 %mul.143 = f32[2,4096,256]{2,1,0:T(8,128)} reshape(f32[2,32,128,2,128]{4,3,2,1,0:T(2,128)} %mul.142) | data formatting | bytes 16777216 | tf_op jit(solution)/shard_map/mul | solution.py:24
  390.0 5.4 mul.158
  395.5 11.5 %mul.159 = f32[2,4096,256]{2,1,0:T(8,128)} reshape(f32[2,32,128,2,128]{4,3,2,1,0:T(2,128)} %mul.158) | data formatting | bytes 16777216 | tf_op jit(solution)/shard_map/mul | solution.py:24
  407.0 1.7 broadcast_select_fusion.1
  408.7 1.3 copy-done.2
  409.9 10.6 %fusion = (bf16[2,4096,256]{2,1,0:T(8,128)(2,1)}, bf16[1,2,4096,256]{3,2,1,0:T(8,128)(2,1)}, bf16[2,4096,256]{2,1,0:T(8,128)(2,1)}) fusion(f32[2,4096,256]{2,1,0:T(8,128)} %mul.159, bf16[1,2,4096,256]{3,2,1,0:T(8,128)(2,1)} %collective-permute-done, bf16[1,2,4096,256]{3,2,1,0:T(8,128)(2,1)S(1)} %copy-done.2, pred[]{:T(512)S(6)} %eq.251, f32[2,4096,256]{2,1,0:T(8,128)} %mul.143), kind=kLoop, calls=%fused_computation.1 | loop fusion | flops 14680064 | bytes 37748736 | tf_op jit(solution)/shard_map/convert_element_type | solution.py:25
  420.5 75.5 %all-to-all-start = ((bf16[4,64,2,4096]{3,2,0,1:T(2,128)(2,1)}), bf16[4,64,2,4096]{3,2,0,1:T(2,128)(2,1)}, u32[]{:S(2)}, u32[]{:S(2)}) async-start(bf16[4,64,2,4096]{3,2,0,1:T(2,128)(2,1)} %copy.39), calls=%async_computation | async-start | bytes 8388608 | tf_op jit(solution)/shard_map/all_to_all | solution.py:96
  496.0 9.7 %copy.45 = bf16[4,64,2,4096]{3,2,1,0:T(2,128)(2,1)} copy(bf16[4,64,2,4096]{3,2,0,1:T(2,128)(2,1)} %all-to-all-done.2) | data formatting | bytes 8388608 | tf_op jit(solution)/shard_map/all_to_all | solution.py:96
  505.8 7.4 reshape.190
  513.1 4.1 fusion.6
  517.2 2.6 mul.163
  519.8 11.9 %convolution_convert_fusion = bf16[512,4096]{1,0:T(8,128)(2,1)} fusion(f32[32,8,32,128]{3,2,1,0:T(8,128)} %bitcast.101, bf16[1,256,4096]{2,1,0:T(8,128)(2,1)} %broadcast_select_fusion.1, f32[512,256]{1,0:T(8,128)S(1)} %fusion.6, bf16[512,4096]{1,0:T(8,128)(2,1)} %reshape.190, bf16[2,4096,256]{2,1,0:T(8,128)(2,1)} %get-tuple-element.6), kind=kOutput, calls=%fused_computation.4 | convolution fusion | flops 2153512960 | bytes 17301504 | tf_op jit(solution)/shard_map/dot_general | solution.py:43
  531.7 7.6 %convert_element_type.200 = bf16[4,64,2,4096]{3,2,1,0:T(2,128)(2,1)} reshape(bf16[512,4096]{1,0:T(8,128)(2,1)} %convolution_convert_fusion) | data formatting | bytes 8388608 | tf_op jit(solution)/shard_map/convert_element_type | solution.py:67
  539.4 7.1 copy.47
  546.5 44.4 %all-to-all-done = bf16[4,64,2,4096]{3,2,0,1:T(2,128)(2,1)} async-done(((bf16[4,64,2,4096]{3,2,0,1:T(2,128)(2,1)}), bf16[4,64,2,4096]{3,2,0,1:T(2,128)(2,1)}, u32[]{:S(2)}, u32[]{:S(2)}) %all-to-all-start) | async-done | bytes 4194336 | tf_op jit(solution)/shard_map/all_to_all | solution.py:96
  590.9 9.7 %copy.40 = bf16[4,64,2,4096]{3,2,1,0:T(2,128)(2,1)} copy(bf16[4,64,2,4096]{3,2,0,1:T(2,128)(2,1)} %all-to-all-done) | data formatting | bytes 8388608 | tf_op jit(solution)/shard_map/all_to_all | solution.py:96
  600.6 7.4 %reshape.186 = bf16[512,4096]{1,0:T(8,128)(2,1)} reshape(bf16[4,64,2,4096]{3,2,1,0:T(2,128)(2,1)} %copy.40) | data formatting | bytes 8388608 | tf_op jit(solution)/shard_map/reshape | solution.py:98
  608.0 4.1 fusion.9
  612.1 2.6 mul.147
  614.7 11.4 %convolution_convert_fusion.2 = bf16[512,4096]{1,0:T(8,128)(2,1)} fusion(f32[32,8,32,128]{3,2,1,0:T(8,128)} %bitcast.102, bf16[1,256,4096]{2,1,0:T(8,128)(2,1)S(1)} %copy-done.1, bf16[512,4096]{1,0:T(8,128)(2,1)} %reshape.186, bf16[2,4096,256]{2,1,0:T(8,128)(2,1)} %get-tuple-element.12, f32[512,256]{1,0:T(8,128)S(1)} %fusion.9), kind=kOutput, calls=%fused_computation.6 | convolution fusion | flops 2153512960 | bytes 17301504 | tf_op jit(solution)/shard_map/dot_general | solution.py:43
  626.1 7.7 %convert_element_type.179 = bf16[4,64,2,4096]{3,2,1,0:T(2,128)(2,1)} reshape(bf16[512,4096]{1,0:T(8,128)(2,1)} %convolution_convert_fusion.2) | data formatting | bytes 8388608 | tf_op jit(solution)/shard_map/convert_element_type | solution.py:67
  633.8 7.0 copy.42
  640.9 3.3 copy.48
  644.2 7.1 all-to-all-start.3
  651.3 35.9 %reduce-scatter.3.cloned.1.call-done = bf16[1,64,2,4096]{3,1,2,0:T(8,128)(2,1)} async-done(((bf16[4,64,2,4096]{3,1,2,0:T(8,128)(2,1)}), bf16[1,64,2,4096]{3,1,2,0:T(8,128)(2,1)}) %reduce-scatter.3.cloned.1.call-update) | async-done | bytes 1048592 | tf_op jit(solution)/shard_map/reduce_scatter | solution.py:66
  687.1 3.3 copy.43
  690.5 10.8 %all-to-all-start.1 = ((bf16[1,64,2,4096]{3,2,0,1:T(2,128)(2,1)}), bf16[1,64,2,4096]{3,2,0,1:T(2,128)(2,1)S(1)}, u32[]{:S(2)}, u32[]{:S(2)}) async-start(bf16[1,64,2,4096]{3,2,0,1:T(2,128)(2,1)} %copy.43), calls=%async_computation.2 | async-start | bytes 2097152 | tf_op jit(solution)/shard_map/all_to_all | solution.py:69
  703.8 1.2 convolution_convert_fusion.4
  704.9 24.4 %all-to-all-done.1 = bf16[1,64,2,4096]{3,2,0,1:T(2,128)(2,1)S(1)} async-done(((bf16[1,64,2,4096]{3,2,0,1:T(2,128)(2,1)}), bf16[1,64,2,4096]{3,2,0,1:T(2,128)(2,1)S(1)}, u32[]{:S(2)}, u32[]{:S(2)}) %all-to-all-start.1) | async-done | bytes 1048608 | tf_op jit(solution)/shard_map/all_to_all | solution.py:69
  729.8 1.2 convolution_convert_fusion.5
  (73 shorter events, 9.7 us)
Async XLA Ops:
  7.2 695.7 %copy-start = (f32[8,8]{1,0:T(8,128)S(1)}, f32[8,8]{1,0:T(8,128)}, u32[]{:S(2)}) copy-start(f32[8,8]{1,0:T(8,128)} %param.18) | copy-start | bytes 772
  54.1 23.9 %copy-start.1 = (bf16[1,256,4096]{2,1,0:T(8,128)(2,1)S(1)}, bf16[1,256,4096]{2,1,0:T(8,128)(2,1)}, u32[]{:S(2)}) copy-start(bf16[1,256,4096]{2,1,0:T(8,128)(2,1)} %param.24) | copy-start | bytes 6291460
  54.1 24.0 %copy-start.6 = (bf16[1,2,32,2]{2,3,1,0:T(2,128)(2,1)S(1)}, bf16[1,2,32,2]{2,3,1,0:T(2,128)(2,1)}, u32[]{:S(2)}) copy-start(bf16[1,2,32,2]{2,3,1,0:T(2,128)(2,1)} %param.23) | copy-start | bytes 772
  54.1 29.3 %copy-start.7 = (bf16[1,2,32]{2,1,0:T(2,128)(2,1)S(1)}, bf16[1,2,32]{2,1,0:T(2,128)(2,1)}, u32[]{:S(2)}) copy-start(bf16[1,2,32]{2,1,0:T(2,128)(2,1)} %param.25) | copy-start | bytes 388
  54.1 29.4 %copy-start.4 = (s32[8,8]{1,0:T(8,128)S(1)}, s32[8,8]{1,0:T(8,128)}, u32[]{:S(2)}) copy-start(s32[8,8]{1,0:T(8,128)} %param.15) | copy-start | bytes 772
  54.1 39.5 %copy-start.5 = (s32[64]{0:T(128)S(1)}, s32[64]{0:T(128)}, u32[]{:S(2)}) copy-start(s32[64]{0:T(128)} %param.20) | copy-start | bytes 772
  54.1 366.4 %all-to-all-start.2 = ((bf16[4,64,2,4096]{3,2,0,1:T(2,128)(2,1)}), bf16[4,64,2,4096]{3,2,0,1:T(2,128)(2,1)}, u32[]{:S(2)}, u32[]{:S(2)}) async-start(bf16[4,64,2,4096]{3,2,0,1:T(2,128)(2,1)} %copy.44), calls=%async_computation.3 | async-start | bytes 8388608 | tf_op jit(solution)/shard_map/all_to_all | solution.py:96
  72.6 336.1 %collective-permute-start = (bf16[1,2,4096,256]{3,2,1,0:T(8,128)(2,1)}, bf16[1,2,4096,256]{3,2,1,0:T(8,128)(2,1)}, u32[]{:S(2)}, u32[]{:S(2)}) collective-permute-start(bf16[1,2,4096,256]{3,2,1,0:T(8,128)(2,1)} %param.22), channel_id=1, source_target_pairs={{0,128},{128,0},{4,132},{132,4},{8,136},{136,8},{12,140},{140,12},... | collective-permute-start | bytes 12582920 | tf_op jit(solution)/shard_map/ppermute | solution.py:14
  78.0 329.0 %collective-permute-start.2 = (bf16[1,256,4096]{2,1,0:T(8,128)(2,1)S(1)}, bf16[1,256,4096]{2,1,0:T(8,128)(2,1)}, u32[]{:S(2)}, u32[]{:S(2)}) collective-permute-start(bf16[1,256,4096]{2,1,0:T(8,128)(2,1)S(1)} %copy-done.1), channel_id=1, source_target_pairs={{0,128},{128,0},{4,132},{132,4},{8,136},{136,8},{12,140},{140,12},... | collective-permute-start | bytes 6291464 | tf_op jit(solution)/shard_map/ppermute | solution.py:14
  78.2 294.2 %collective-permute-start.1 = (bf16[1,2,32,2]{2,3,1,0:T(2,128)(2,1)S(1)}, bf16[1,2,32,2]{2,3,1,0:T(2,128)(2,1)S(1)}, u32[]{:S(2)}, u32[]{:S(2)}) collective-permute-start(bf16[1,2,32,2]{2,3,1,0:T(2,128)(2,1)S(1)} %copy-done.6), channel_id=1, source_target_pairs={{0,128},{128,0},{4,132},{132,4},{8,136},{136,8},{12,140},{140,12},... | collective-permute-start | bytes 776 | tf_op jit(solution)/shard_map/ppermute | solution.py:14
  83.4 288.4 %collective-permute-start.3 = (bf16[1,2,32]{2,1,0:T(2,128)(2,1)S(1)}, bf16[1,2,32]{2,1,0:T(2,128)(2,1)S(1)}, u32[]{:S(2)}, u32[]{:S(2)}) collective-permute-start(bf16[1,2,32]{2,1,0:T(2,128)(2,1)S(1)} %copy-done.7), channel_id=1, source_target_pairs={{0,128},{128,0},{4,132},{132,4},{8,136},{136,8},{12,140},{140,12},... | collective-permute-start | bytes 392 | tf_op jit(solution)/shard_map/ppermute | solution.py:14
  116.8 10.2 %copy-start.9 = (s32[64]{0:T(128)S(1)}, s32[64]{0:T(128)}, u32[]{:S(2)}) copy-start(s32[64]{0:T(128)} %param.21) | copy-start | bytes 772
  407.0 2.9 copy-start.2
  420.5 170.4 %all-to-all-start = ((bf16[4,64,2,4096]{3,2,0,1:T(2,128)(2,1)}), bf16[4,64,2,4096]{3,2,0,1:T(2,128)(2,1)}, u32[]{:S(2)}, u32[]{:S(2)}) async-start(bf16[4,64,2,4096]{3,2,0,1:T(2,128)(2,1)} %copy.39), calls=%async_computation | async-start | bytes 8388608 | tf_op jit(solution)/shard_map/all_to_all | solution.py:96
  496.0 144.9 %reduce-scatter.5.cloned.1.call-start = ((), (), s32[]{:S(2)}) async-start(), calls=%async_computation.7 | async-start | bytes 5242880 | tf_op jit(solution)/shard_map/reduce_scatter | solution.py:66
  546.4 140.7 %reduce-scatter.3.cloned.1.call-start = ((), (), s32[]{:S(2)}) async-start(), calls=%async_computation.6 | async-start | bytes 5242880 | tf_op jit(solution)/shard_map/reduce_scatter | solution.py:66
  640.8 60.4 %copy-start.3 = (s32[8,8]{1,0:T(8,128)S(1)}, s32[8,8]{1,0:T(8,128)}, u32[]{:S(2)}) copy-start(s32[8,8]{1,0:T(8,128)} %param.16) | copy-start | bytes 772
  640.8 62.3 %copy-start.8 = (f32[8,8]{1,0:T(8,128)S(1)}, f32[8,8]{1,0:T(8,128)}, u32[]{:S(2)}) copy-start(f32[8,8]{1,0:T(8,128)} %param.17) | copy-start | bytes 772
  644.2 46.3 %all-to-all-start.3 = ((bf16[1,64,2,4096]{3,2,0,1:T(2,128)(2,1)}), bf16[1,64,2,4096]{3,2,0,1:T(2,128)(2,1)S(1)}, u32[]{:S(2)}, u32[]{:S(2)}) async-start(bf16[1,64,2,4096]{3,2,0,1:T(2,128)(2,1)} %copy.48), calls=%async_computation.5 | async-start | bytes 2097152 | tf_op jit(solution)/shard_map/all_to_all | solution.py:69
  690.5 38.9 %all-to-all-start.1 = ((bf16[1,64,2,4096]{3,2,0,1:T(2,128)(2,1)}), bf16[1,64,2,4096]{3,2,0,1:T(2,128)(2,1)S(1)}, u32[]{:S(2)}, u32[]{:S(2)}) async-start(bf16[1,64,2,4096]{3,2,0,1:T(2,128)(2,1)} %copy.43), calls=%async_computation.2 | async-start | bytes 2097152 | tf_op jit(solution)/shard_map/all_to_all | solution.py:69
Sparse Core Ops, SparseCore 0:
  546.6 49.7 reduce-scatter.4
  640.9 46.1 reduce-scatter.2
where the time goes:
time: 749 us; the launch traced here: 738 us
  waiting for transfers between devices  348 us (46%)
  local copies, waits for them, and re-layouts  148 us (20%)
  starting transfers between devices  123 us (16%)
  matrix products  40.9 us (5%)
  blocking collectives  40.4 us (5%)
  other arithmetic  22.3 us (3%)
  between operations  15.4 us (2%)
    ppermute x4, waiting for transfers between devices, partner(): return lax.ppermute(block, axis, route)  244 us
    all_to_all x2, starting transfers between devices, decode_step(): lax.all_to_all(outgoing, 'expert', split_axis=1, concat_axis=1, tiled=True)  93.9 us
    all_to_all x2, waiting for transfers between devices, decode_step(): lax.all_to_all(outgoing, 'expert', split_axis=1, concat_axis=1, tiled=True)  44.4 us
    mul x6, local copies, waits for them, and re-layouts, dequantize(): scaled = blocked * scales.astype(jnp.float32)[..., :, None, :, None]  39 us
    reduce_scatter x2, waiting for transfers between devices, finish(): lax.psum_scatter(partial_terms.astype(jnp.bfloat16), 'replica', scatter_d...  35.9 us
    reshape x4, local copies, waits for them, and re-layouts, decode_step(): outgoing.astype(jnp.bfloat16).reshape(copies, experts, capacity, features)  35.8 us
    convert_element_type x4, local copies, waits for them, and re-layouts, finish(): partial_terms.astype(jnp.bfloat16)  29.4 us
    all_to_all x2, waiting for transfers between devices, finish(): lax.all_to_all(summed, 'expert', split_axis=1, concat_axis=1, tiled=True)  24.4 us
  transfers between devices with their start and end apart: 10, of which 4 were waited for; matrix products, arithmetic and copies ran while one was open for 25% of the time, Pallas kernels for 0%

commit v1 on v0

--- a/solution.py
+++ b/solution.py
@@ -66,7 +66,15 @@
     summed = lax.psum_scatter(
         partial_terms.astype(jnp.bfloat16), "replica", scatter_dimension=0, tiled=True
     )
-    return lax.all_to_all(summed, "expert", split_axis=1, concat_axis=1, tiled=True)
+    return jnp.concatenate(
+        lax.all_to_all(
+            jnp.stack(jnp.split(summed, lax.axis_size("expert"), 1)),
+            axis_name="expert",
+            split_axis=0,
+            concat_axis=0,
+        ),
+        axis=1,
+    )
 
 
 def decode_step(hidden, routes, mixing, norm_gain, owner_slots, weights):

time: 749 us -> 803 us (1.072)
  local copies, waits for them, and re-layouts: 148 us -> 238 us
  waiting for transfers between devices: 348 us -> 312 us
    unnamed x20 -> x150, local copies, waits for them, and re-layouts: 1.32 us -> 80.2 us
    reduce_scatter x2, waiting for transfers between devices: 35.9 us -> 0.04 us  [finish(): lax.psum_scatter(partial_terms.astype(jnp.bfloat16), 'replica', scatter_d...]
    split x0 -> x8, local copies, waits for them, and re-layouts: none -> 16.6 us  [finish(): jnp.split(summed, lax.axis_size('expert'), 1)]
  transfers between devices with their start and end apart: 10 -> 10, of which waited for: 4 -> 3; matrix products, arithmetic and copies ran while one was open for 25% -> 34% of each run, Pallas kernels for 0% -> 0%
where the time goes in v1:
time: 803 us; the launch traced here: 792 us
  waiting for transfers between devices  312 us (39%)
  local copies, waits for them, and re-layouts  238 us (30%)
  starting transfers between devices  123 us (15%)
  matrix products  40.9 us (5%)
  blocking collectives  40.4 us (5%)
  other arithmetic  22.3 us (3%)
  between operations  15.6 us (2%)
    ppermute x4, waiting for transfers between devices, partner(): return lax.ppermute(block, axis, route)  244 us
    all_to_all x2, starting transfers between devices, decode_step(): lax.all_to_all(outgoing, 'expert', split_axis=1, concat_axis=1, tiled=True)  93.9 us
    unnamed x150, local copies, waits for them, and re-layouts  80.2 us
    all_to_all x2, waiting for transfers between devices, decode_step(): lax.all_to_all(outgoing, 'expert', split_axis=1, concat_axis=1, tiled=True)  44.2 us
    mul x6, local copies, waits for them, and re-layouts, dequantize(): scaled = blocked * scales.astype(jnp.float32)[..., :, None, :, None]  39 us
    reshape x4, local copies, waits for them, and re-layouts, decode_step(): outgoing.astype(jnp.bfloat16).reshape(copies, experts, capacity, features)  35.8 us
    convert_element_type x4, local copies, waits for them, and re-layouts, finish(): partial_terms.astype(jnp.bfloat16)  29.6 us
    all_to_all x2, waiting for transfers between devices, finish(): lax.all_to_all(jnp.stack(jnp.split(summed, lax.axis_size('expert'), 1)),...  24.4 us
  transfers between devices with their start and end apart: 10, of which 3 were waited for; matrix products, arithmetic and copies ran while one was open for 34% of the time, Pallas kernels for 0%

profile of v1, /device:TPU:1, one launch (start us, length us, event | category | flops | bytes accessed | tf_op | source)
XLA Modules:
  0.0 792.4 jit_solution(9742034736337061482)
XLA Ops:
  8.7 10.4 %all_gather.14 = s32[32,8]{1,0:T(8,128)S(1)} all-gather(s32[8,8]{1,0:T(8,128)} %param.16), channel_id=1, replica_groups=mesh['expert'=64,'replica'=4] {'replica'}, dimensions={0}, use_global_device_ids=true | all-gather | bytes 1280 | tf_op jit(solution)/shard_map/all_gather | solution.py:90
  23.6 9.4 %all_gather.15 = bf16[32,4096]{1,0:T(8,128)(2,1)S(1)} all-gather(bf16[8,4096]{1,0:T(8,128)(2,1)S(1)} %get-tuple-element.141), channel_id=1, replica_groups=mesh['expert'=64,'replica'=4] {'replica'}, dimensions={0}, use_global_device_ids=true | all-gather | bytes 327680 | tf_op jit(solution)/shard_map/all_gather | solution.py:89
  33.0 3.3 convolution_convert_fusion.1
  36.3 7.6 reshape.182
  43.9 10.2 %copy.354 = bf16[4,64,2,4096]{3,2,0,1:T(2,128)(2,1)} copy(bf16[4,64,2,4096]{3,2,1,0:T(2,128)(2,1)} %reshape.182) | data formatting | bytes 8388608 | tf_op jit(solution)/shard_map/reshape | solution.py:103
  54.1 18.4 %all-to-all-start.2 = ((bf16[4,64,2,4096]{3,2,0,1:T(2,128)(2,1)}), bf16[4,64,2,4096]{3,2,0,1:T(2,128)(2,1)}, u32[]{:S(2)}, u32[]{:S(2)}) async-start(bf16[4,64,2,4096]{3,2,0,1:T(2,128)(2,1)} %copy.354), calls=%async_computation.3 | async-start | bytes 8388608 | tf_op jit(solution)/shard_map/all_to_all | solution.py:104
  72.6 5.5 collective-permute-start
  78.2 5.3 collective-permute-start.1
  83.5 10.1 %all_gather.12 = s32[32,8]{1,0:T(8,128)S(1)} all-gather(s32[8,8]{1,0:T(8,128)S(1)} %copy-done.6), channel_id=1, replica_groups=mesh['expert'=64,'replica'=4] {'replica'}, dimensions={0}, use_global_device_ids=true | all-gather | bytes 1280 | tf_op jit(solution)/shard_map/all_gather | solution.py:90
  94.9 10.6 %all_gather.13 = bf16[32,4096]{1,0:T(8,128)(2,1)S(1)} all-gather(bf16[8,4096]{1,0:T(8,128)(2,1)S(1)} %get-tuple-element.142), channel_id=1, replica_groups=mesh['expert'=64,'replica'=4] {'replica'}, dimensions={0}, use_global_device_ids=true | all-gather | bytes 327680 | tf_op jit(solution)/shard_map/all_gather | solution.py:89
  105.6 3.3 convolution_convert_fusion.3
  108.9 7.8 reshape.179
  116.8 10.2 %copy.287 = bf16[4,64,2,4096]{3,2,0,1:T(2,128)(2,1)} copy(bf16[4,64,2,4096]{3,2,1,0:T(2,128)(2,1)} %reshape.179) | data formatting | bytes 8388608 | tf_op jit(solution)/shard_map/reshape | solution.py:103
  128.2 243.6 %collective-permute-done.3 = bf16[1,2,32]{2,1,0:T(2,128)(2,1)S(1)} collective-permute-done((bf16[1,2,32]{2,1,0:T(2,128)(2,1)S(1)}, bf16[1,2,32]{2,1,0:T(2,128)(2,1)S(1)}, u32[]{:S(2)}, u32[]{:S(2)}) %collective-permute-start.3) | collective-permute-done | bytes 160 | tf_op jit(solution)/shard_map/ppermute | solution.py:14
  373.0 5.4 mul.142
  378.5 11.5 %mul.143 = f32[2,4096,256]{2,1,0:T(8,128)} reshape(f32[2,32,128,2,128]{4,3,2,1,0:T(2,128)} %mul.142) | data formatting | bytes 16777216 | tf_op jit(solution)/shard_map/mul | solution.py:24
  390.0 5.4 mul.158
  395.5 11.5 %mul.159 = f32[2,4096,256]{2,1,0:T(8,128)} reshape(f32[2,32,128,2,128]{4,3,2,1,0:T(2,128)} %mul.158) | data formatting | bytes 16777216 | tf_op jit(solution)/shard_map/mul | solution.py:24
  407.0 1.7 broadcast_select_fusion.1
  408.7 1.3 copy-done.2
  409.9 10.6 %fusion = (bf16[2,4096,256]{2,1,0:T(8,128)(2,1)}, bf16[1,2,4096,256]{3,2,1,0:T(8,128)(2,1)}, bf16[2,4096,256]{2,1,0:T(8,128)(2,1)}) fusion(f32[2,4096,256]{2,1,0:T(8,128)} %mul.159, bf16[1,2,4096,256]{3,2,1,0:T(8,128)(2,1)} %collective-permute-done, bf16[1,2,4096,256]{3,2,1,0:T(8,128)(2,1)S(1)} %copy-done.2, pred[]{:T(512)S(6)} %eq.251, f32[2,4096,256]{2,1,0:T(8,128)} %mul.143), kind=kLoop, calls=%fused_computation.1 | loop fusion | flops 14680064 | bytes 37748736 | tf_op jit(solution)/shard_map/convert_element_type | solution.py:25
  420.5 75.5 %all-to-all-start = ((bf16[4,64,2,4096]{3,2,0,1:T(2,128)(2,1)}), bf16[4,64,2,4096]{3,2,0,1:T(2,128)(2,1)}, u32[]{:S(2)}, u32[]{:S(2)}) async-start(bf16[4,64,2,4096]{3,2,0,1:T(2,128)(2,1)} %copy.287), calls=%async_computation | async-start | bytes 8388608 | tf_op jit(solution)/shard_map/all_to_all | solution.py:104
  496.0 9.7 %copy.355 = bf16[4,64,2,4096]{3,2,1,0:T(2,128)(2,1)} copy(bf16[4,64,2,4096]{3,2,0,1:T(2,128)(2,1)} %all-to-all-done.2) | data formatting | bytes 8388608 | tf_op jit(solution)/shard_map/all_to_all | solution.py:104
  505.8 7.4 reshape.183
  513.1 4.1 fusion.6
  517.2 2.6 mul.163
  519.8 11.9 %convolution_convert_fusion = bf16[512,4096]{1,0:T(8,128)(2,1)} fusion(f32[32,8,32,128]{3,2,1,0:T(8,128)} %bitcast.605, bf16[1,256,4096]{2,1,0:T(8,128)(2,1)} %broadcast_select_fusion.1, f32[512,256]{1,0:T(8,128)S(1)} %fusion.6, bf16[512,4096]{1,0:T(8,128)(2,1)} %reshape.183, bf16[2,4096,256]{2,1,0:T(8,128)(2,1)} %get-tuple-element.6), kind=kOutput, calls=%fused_computation.4 | convolution fusion | flops 2153512960 | bytes 17301504 | tf_op jit(solution)/shard_map/dot_general | solution.py:43
  531.7 7.6 convert_element_type.200
  539.4 7.1 copy.357
  546.7 44.2 %all-to-all-done = bf16[4,64,2,4096]{3,2,0,1:T(2,128)(2,1)} async-done(((bf16[4,64,2,4096]{3,2,0,1:T(2,128)(2,1)}), bf16[4,64,2,4096]{3,2,0,1:T(2,128)(2,1)}, u32[]{:S(2)}, u32[]{:S(2)}) %all-to-all-start) | async-done | bytes 4194336 | tf_op jit(solution)/shard_map/all_to_all | solution.py:104
  590.9 9.7 %copy.288 = bf16[4,64,2,4096]{3,2,1,0:T(2,128)(2,1)} copy(bf16[4,64,2,4096]{3,2,0,1:T(2,128)(2,1)} %all-to-all-done) | data formatting | bytes 8388608 | tf_op jit(solution)/shard_map/all_to_all | solution.py:104
  600.6 7.2 reshape.180
  607.8 4.1 fusion.9
  611.9 2.6 mul.147
  614.5 11.4 %convolution_convert_fusion.2 = bf16[512,4096]{1,0:T(8,128)(2,1)} fusion(f32[32,8,32,128]{3,2,1,0:T(8,128)} %bitcast.606, bf16[1,256,4096]{2,1,0:T(8,128)(2,1)S(1)} %copy-done.1, bf16[512,4096]{1,0:T(8,128)(2,1)} %reshape.180, bf16[2,4096,256]{2,1,0:T(8,128)(2,1)} %get-tuple-element.12, f32[512,256]{1,0:T(8,128)S(1)} %fusion.9), kind=kOutput, calls=%fused_computation.6 | convolution fusion | flops 2153512960 | bytes 17301504 | tf_op jit(solution)/shard_map/dot_general | solution.py:43
  625.9 7.9 convert_element_type.179
  633.8 7.0 copy.290
  640.9 1.7 fusion.46
  647.0 3.1 fusion.45
  662.0 3.0 fusion.44
  689.5 7.2 all-to-all-start.3
  696.8 1.7 fusion.50
  702.9 3.0 fusion.49
  717.8 2.8 fusion.48
  745.0 10.3 %all-to-all-start.1 = ((bf16[64,1,1,2,4096]{4,3,2,1,0:T(2,128)(2,1)}), bf16[64,1,1,2,4096]{4,3,2,1,0:T(2,128)(2,1)S(1)}, u32[]{:S(2)}, u32[]{:S(2)}) async-start(bf16[64,1,1,2,4096]{4,3,2,1,0:T(2,128)(2,1)} %constant_dynamic-update-slice_fusion), calls=%async_computation.2 | async-start | bytes 2097152 | tf_op jit(solution)/shard_map/all_to_all | solution.py:70
  757.9 1.2 convolution_convert_fusion.4
  759.1 24.4 %all-to-all-done.1 = bf16[64,1,1,2,4096]{4,3,2,1,0:T(2,128)(2,1)S(1)} async-done(((bf16[64,1,1,2,4096]{4,3,2,1,0:T(2,128)(2,1)}), bf16[64,1,1,2,4096]{4,3,2,1,0:T(2,128)(2,1)S(1)}, u32[]{:S(2)}, u32[]{:S(2)}) %all-to-all-start.1) | async-done | bytes 1048608 | tf_op jit(solution)/shard_map/all_to_all | solution.py:70
  783.9 1.2 convolution_convert_fusion.5
  (211 shorter events, 94.3 us)
Async XLA Ops:
  7.2 749.8 %copy-start = (f32[8,8]{1,0:T(8,128)S(1)}, f32[8,8]{1,0:T(8,128)}, u32[]{:S(2)}) copy-start(f32[8,8]{1,0:T(8,128)} %param.18) | copy-start | bytes 772
  54.1 23.9 %copy-start.1 = (bf16[1,256,4096]{2,1,0:T(8,128)(2,1)S(1)}, bf16[1,256,4096]{2,1,0:T(8,128)(2,1)}, u32[]{:S(2)}) copy-start(bf16[1,256,4096]{2,1,0:T(8,128)(2,1)} %param.24) | copy-start | bytes 6291460
  54.1 24.0 %copy-start.8 = (bf16[1,2,32,2]{2,3,1,0:T(2,128)(2,1)S(1)}, bf16[1,2,32,2]{2,3,1,0:T(2,128)(2,1)}, u32[]{:S(2)}) copy-start(bf16[1,2,32,2]{2,3,1,0:T(2,128)(2,1)} %param.23) | copy-start | bytes 772
  54.1 29.3 %copy-start.9 = (bf16[1,2,32]{2,1,0:T(2,128)(2,1)S(1)}, bf16[1,2,32]{2,1,0:T(2,128)(2,1)}, u32[]{:S(2)}) copy-start(bf16[1,2,32]{2,1,0:T(2,128)(2,1)} %param.25) | copy-start | bytes 388
  54.1 29.4 %copy-start.6 = (s32[8,8]{1,0:T(8,128)S(1)}, s32[8,8]{1,0:T(8,128)}, u32[]{:S(2)}) copy-start(s32[8,8]{1,0:T(8,128)} %param.15) | copy-start | bytes 772
  54.1 39.5 %copy-start.7 = (s32[64]{0:T(128)S(1)}, s32[64]{0:T(128)}, u32[]{:S(2)}) copy-start(s32[64]{0:T(128)} %param.20) | copy-start | bytes 772
  54.1 366.4 %all-to-all-start.2 = ((bf16[4,64,2,4096]{3,2,0,1:T(2,128)(2,1)}), bf16[4,64,2,4096]{3,2,0,1:T(2,128)(2,1)}, u32[]{:S(2)}, u32[]{:S(2)}) async-start(bf16[4,64,2,4096]{3,2,0,1:T(2,128)(2,1)} %copy.354), calls=%async_computation.3 | async-start | bytes 8388608 | tf_op jit(solution)/shard_map/all_to_all | solution.py:104
  72.6 336.1 %collective-permute-start = (bf16[1,2,4096,256]{3,2,1,0:T(8,128)(2,1)}, bf16[1,2,4096,256]{3,2,1,0:T(8,128)(2,1)}, u32[]{:S(2)}, u32[]{:S(2)}) collective-permute-start(bf16[1,2,4096,256]{3,2,1,0:T(8,128)(2,1)} %param.22), channel_id=1, source_target_pairs={{0,128},{128,0},{4,132},{132,4},{8,136},{136,8},{12,140},{140,12},... | collective-permute-start | bytes 12582920 | tf_op jit(solution)/shard_map/ppermute | solution.py:14
  78.0 329.0 %collective-permute-start.2 = (bf16[1,256,4096]{2,1,0:T(8,128)(2,1)S(1)}, bf16[1,256,4096]{2,1,0:T(8,128)(2,1)}, u32[]{:S(2)}, u32[]{:S(2)}) collective-permute-start(bf16[1,256,4096]{2,1,0:T(8,128)(2,1)S(1)} %copy-done.1), channel_id=1, source_target_pairs={{0,128},{128,0},{4,132},{132,4},{8,136},{136,8},{12,140},{140,12},... | collective-permute-start | bytes 6291464 | tf_op jit(solution)/shard_map/ppermute | solution.py:14
  78.2 294.2 %collective-permute-start.1 = (bf16[1,2,32,2]{2,3,1,0:T(2,128)(2,1)S(1)}, bf16[1,2,32,2]{2,3,1,0:T(2,128)(2,1)S(1)}, u32[]{:S(2)}, u32[]{:S(2)}) collective-permute-start(bf16[1,2,32,2]{2,3,1,0:T(2,128)(2,1)S(1)} %copy-done.8), channel_id=1, source_target_pairs={{0,128},{128,0},{4,132},{132,4},{8,136},{136,8},{12,140},{140,12},... | collective-permute-start | bytes 776 | tf_op jit(solution)/shard_map/ppermute | solution.py:14
  83.4 288.4 %collective-permute-start.3 = (bf16[1,2,32]{2,1,0:T(2,128)(2,1)S(1)}, bf16[1,2,32]{2,1,0:T(2,128)(2,1)S(1)}, u32[]{:S(2)}, u32[]{:S(2)}) collective-permute-start(bf16[1,2,32]{2,1,0:T(2,128)(2,1)S(1)} %copy-done.9), channel_id=1, source_target_pairs={{0,128},{128,0},{4,132},{132,4},{8,136},{136,8},{12,140},{140,12},... | collective-permute-start | bytes 392 | tf_op jit(solution)/shard_map/ppermute | solution.py:14
  116.8 10.2 %copy-start.11 = (s32[64]{0:T(128)S(1)}, s32[64]{0:T(128)}, u32[]{:S(2)}) copy-start(s32[64]{0:T(128)} %param.21) | copy-start | bytes 772
  407.0 2.9 copy-start.2
  420.5 170.4 %all-to-all-start = ((bf16[4,64,2,4096]{3,2,0,1:T(2,128)(2,1)}), bf16[4,64,2,4096]{3,2,0,1:T(2,128)(2,1)}, u32[]{:S(2)}, u32[]{:S(2)}) async-start(bf16[4,64,2,4096]{3,2,0,1:T(2,128)(2,1)} %copy.287), calls=%async_computation | async-start | bytes 8388608 | tf_op jit(solution)/shard_map/all_to_all | solution.py:104
  496.0 144.9 %reduce-scatter.5.cloned.1.call-start = ((), (), s32[]{:S(2)}) async-start(), calls=%async_computation.7 | async-start | bytes 5242880 | tf_op jit(solution)/shard_map/reduce_scatter | solution.py:66
  546.4 150.3 %reduce-scatter.3.cloned.1.call-start = ((), (), s32[]{:S(2)}) async-start(), calls=%async_computation.6 | async-start | bytes 5242880 | tf_op jit(solution)/shard_map/reduce_scatter | solution.py:66
  640.9 35.4 %copy-start.4 = (bf16[1,64,2,4096]{3,1,2,0:T(8,128)(2,1)S(1)}, bf16[1,64,2,4096]{3,1,2,0:T(8,128)(2,1)}, u32[]{:S(2)}) copy-start(bf16[1,64,2,4096]{3,1,2,0:T(8,128)(2,1)} %reduce-scatter.5.cloned.1.call-done) | copy-start | bytes 3145732
  689.5 55.5 %all-to-all-start.3 = ((bf16[64,1,1,2,4096]{4,3,2,1,0:T(2,128)(2,1)}), bf16[64,1,1,2,4096]{4,3,2,1,0:T(2,128)(2,1)S(1)}, u32[]{:S(2)}, u32[]{:S(2)}) async-start(bf16[64,1,1,2,4096]{4,3,2,1,0:T(2,128)(2,1)} %constant_dynamic-update-slice_fusion.64), calls=%async_computation.5 | async-start | bytes 2097152 | tf_op jit(solution)/shard_map/all_to_all | solution.py:70
  696.8 35.0 %copy-start.3 = (bf16[1,64,2,4096]{3,1,2,0:T(8,128)(2,1)S(1)}, bf16[1,64,2,4096]{3,1,2,0:T(8,128)(2,1)}, u32[]{:S(2)}) copy-start(bf16[1,64,2,4096]{3,1,2,0:T(8,128)(2,1)} %reduce-scatter.3.cloned.1.call-done) | copy-start | bytes 3145732
  702.9 52.5 %copy-start.5 = (s32[8,8]{1,0:T(8,128)S(1)}, s32[8,8]{1,0:T(8,128)}, u32[]{:S(2)}) copy-start(s32[8,8]{1,0:T(8,128)} %param.16) | copy-start | bytes 772
  705.8 51.4 %copy-start.10 = (f32[8,8]{1,0:T(8,128)S(1)}, f32[8,8]{1,0:T(8,128)}, u32[]{:S(2)}) copy-start(f32[8,8]{1,0:T(8,128)} %param.17) | copy-start | bytes 772
  745.0 38.5 %all-to-all-start.1 = ((bf16[64,1,1,2,4096]{4,3,2,1,0:T(2,128)(2,1)}), bf16[64,1,1,2,4096]{4,3,2,1,0:T(2,128)(2,1)S(1)}, u32[]{:S(2)}, u32[]{:S(2)}) async-start(bf16[64,1,1,2,4096]{4,3,2,1,0:T(2,128)(2,1)} %constant_dynamic-update-slice_fusion), calls=%async_computation.2 | async-start | bytes 2097152 | tf_op jit(solution)/shard_map/all_to_all | solution.py:70
Sparse Core Ops, SparseCore 0:
  546.6 49.7 reduce-scatter.4
  641.0 46.1 reduce-scatter.2
